TPU v7x, 256 devices: a whole 4x4x8 slice. The times are simulated.
256 devices in a mesh: seq: 32 (over x, y, core), dp: 8 (over z).
Axes of the slice: x: 4, y: 4, z: 8, core: 2. Of those that a mesh axis runs over, the one named last changes fastest.
Arguments:
- points: bfloat16 [8, 16384, 512], P('dp', 'seq'), may hold values from -6 to 6
- cotangent: bfloat16 [8, 16384, 512], P('dp', 'seq'), may hold values from -6 to 6
- dest: int32 [8, 16384], P('dp', 'seq'), may hold values from 0 to 16383, as said below
- w_qkv: bfloat16 [512, 1536], replicated
- w_proj: bfloat16 [512, 512], replicated, may hold values from -0.25 to 0.25
- gain: float32 [512], replicated, may hold values from 0.5 to 1.5
Outputs:
- grad_points: bfloat16 [8, 16384, 512], P('dp', 'seq')
- grad_qkv: float32 [512, 1536], replicated
- grad_proj: float32 [512, 512], replicated
- gain_gradient: float32 [512], replicated
Inputs may be any that keep to these rules, and one draw needn't show every extreme that they name: For each scan, dest is a permutation of the 16384 positions, one serialization order of the points. Of the 512 points of one device, at most 32 have positions on any one device's range of 512 positions, and exactly 32 for some device.
All inputs are finite; a program needn't handle non-finite values.
Results may differ from a plain program's by a relative error of at most 0.013.
The roundings to bfloat16 on the way count: a program that leaves them out, or rounds other values in their place, can miss the bound.
Values may be sent and summed in bfloat16 or wider, within the bound.
A program may use at most 64 MiB of HBM per device.

v0:
```python
import jax
import jax.numpy as jnp
from jax import lax
from jax.experimental import pallas as pl
from jax.experimental.pallas import tpu as pltpu
from jax.sharding import Mesh
from jax.sharding import PartitionSpec as P

SEQ = ("seq_0", "seq_1", "seq_2")
MESH_ID = pl.DeviceIdType.MESH
F32, BF16 = jnp.float32, jnp.bfloat16
ROWS = 512
C = 512
N_SEQ = 32
CAP = 32
SLOTS = N_SEQ * CAP
HEADS, HD = 8, 64
PAIRS = HEADS // 2
SCALE = 1.0 / HD**0.5
CHUNK = 2048


def nn(a, b):
    return jnp.dot(a, b, preferred_element_type=F32)


def nt(a, b):
    return lax.dot_general(a, b, (((1,), (1,)), ((), ())), preferred_element_type=F32)


def iota(shape, dim):
    return lax.broadcasted_iota(jnp.int32, shape, dim)


def hot(cond):
    return jnp.where(cond, 1.0, 0.0).astype(BF16)


def remote(src, dst, send, recv, device):
    return pltpu.make_async_remote_copy(
        src_ref=src, dst_ref=dst, send_sem=send, recv_sem=recv, device_id=device, device_id_type=MESH_ID
    )


def seq_peer(mx, my, mc, d, sign):
    dx, dy, dc = d // 8, (d // 2) % 4, d % 2
    return {
        "seq_0": lax.rem(mx + (dx if sign > 0 else 4 - dx), 4),
        "seq_1": lax.rem(my + (dy if sign > 0 else 4 - dy), 4),
        "seq_2": lax.rem(mc + dc, 2),
    }


AXES = {"seq_0": 4, "seq_1": 4, "seq_2": 2, "dp": 8}
FAR_FIRST = sorted(range(1, N_SEQ), key=lambda d: -(min(d // 8, 4 - d // 8) + min(d // 2 % 4, 4 - d // 2 % 4)))


def block_kernel(
    dest_ref, pts_hbm, cot_hbm, wqkv_hbm, wproj_hbm, gain_ref,
    out_ref, res, gg_ref,
    send_a, recv_a, send_b, recv_b, back, pos_send, pos_recv, pos_all,
    qkv, dattn, sgrad, xhat, invs, normed_t, dqkv, attn_t, probs, onehot_u, onehot_ut, onehot_pt,
    grads, acc, acc2, acc3, core_buf, first_buf, second_buf, z_buf, g_core, g_x, g_y, g_z,
    pts_ref, cot_ref, wqkv_ref, wproj_ref,
    sem_send, sem_recv, r_send, r_recv, g_send, g_recv, in_sem,
):
    loads = [
        pltpu.make_async_copy(src, dst, in_sem.at[k])
        for k, (src, dst) in enumerate(
            ((pts_hbm, pts_ref), (cot_hbm, cot_ref), (wqkv_hbm, wqkv_ref), (wproj_hbm, wproj_ref))
        )
    ]
    for load in loads:
        load.start()
    me = {a: lax.axis_index(a) for a in AXES}
    mx, my, mc = me["seq_0"], me["seq_1"], me["seq_2"]
    here = dict(me)

    def peers(axis):
        n = AXES[axis]
        return [lax.rem(me[axis] + d, n) for d in range(1, n)]

    barrier = pltpu.get_barrier_semaphore()
    for d in range(1, N_SEQ):
        pl.semaphore_signal(barrier, inc=1, device_id=seq_peer(mx, my, mc, d, 1), device_id_type=MESH_ID)
    for t in peers("dp"):
        pl.semaphore_signal(barrier, inc=1, device_id={"dp": t}, device_id_type=MESH_ID)

    dest = dest_ref[...]
    owner, slot = dest >> 9, dest & 511
    rel = ((((owner >> 3) - mx) & 3) << 3) | ((((owner >> 1) - my) & 3) << 1) | ((owner - mc) & 1)
    to_hot_f = jnp.where(iota((N_SEQ, ROWS), 0) == rel, 1.0, 0.0)
    to_hot = to_hot_f.astype(BF16)
    earlier = hot(iota((ROWS, ROWS), 0) < iota((ROWS, ROWS), 1))
    rank = jnp.sum(to_hot_f * nn(to_hot, earlier), axis=0, keepdims=True).astype(jnp.int32)
    sid = rel * CAP + rank
    rank_hot = hot(iota((128, ROWS), 0) == rank)
    pos_hi = nt((to_hot_f * (slot >> 4).astype(F32)).astype(BF16), rank_hot)
    pos_lo = nt((to_hot_f * (slot & 15).astype(F32)).astype(BF16), rank_hot)
    pos = pos_hi * 16.0 + pos_lo
    for d in range(N_SEQ):
        pos_send[d] = pos[d : d + 1, :]

    def pack(src_ref, send_ref, recv_ref, index, first=None):
        data = src_ref[...]
        for b in (2, 1, 3, 0):
            pick = hot(iota((256, ROWS), 0) + b * 256 == sid)
            send_ref[b * 256 : (b + 1) * 256, :] = nn(pick, data).astype(BF16)
            if first is not None:
                first()
                first = None
            send_all(send_ref, recv_ref, index, 1, [d for d in FAR_FIRST if d // 8 == b])
        recv_ref[0:CAP, :] = send_ref[0:CAP, :]

    def send_all(send_ref, recv_ref, index, sign, order=FAR_FIRST):
        for d in order:
            rows = pl.ds(d * CAP, CAP)
            remote(send_ref.at[rows], recv_ref.at[rows], sem_send.at[index], sem_recv.at[index],
                   seq_peer(mx, my, mc, d, sign)).start()

    def wait_recv(ref, index):
        remote(ref, ref, sem_send.at[index], sem_recv.at[index], here).wait_recv()

    def wait_send(ref, index):
        remote(ref, ref, sem_send.at[index], sem_recv.at[index], here).wait_send()

    def enter():
        pl.semaphore_wait(barrier, N_SEQ - 1 + AXES["dp"] - 1)
        for d in range(1, N_SEQ):
            remote(pos_send.at[d], pos_recv.at[d], sem_send.at[2], sem_recv.at[2],
                   seq_peer(mx, my, mc, d, 1)).start()

    loads[0].wait()
    pack(pts_ref, send_a, recv_a, 0, enter)
    loads[1].wait()
    pack(cot_ref, send_b, recv_b, 1)

    sid_col = jnp.transpose(jnp.broadcast_to(sid.astype(F32), (128, ROWS))).astype(jnp.int32)
    for j in range(SLOTS // 128):
        onehot_pt[:, j * 128 : (j + 1) * 128] = hot(iota((ROWS, 128), 1) + j * 128 == sid_col)

    others = pl.ds(CAP, SLOTS - CAP)
    wait_recv(pos_recv.at[pl.ds(1, N_SEQ - 1)], 2)
    pos_all[0:1, :] = pos_send[0]
    for d in range(1, N_SEQ):
        pos_all[d : d + 1, :] = pos_recv[d]
    got = pos_all[...].astype(jnp.int32)
    spread = hot(iota((128, SLOTS), 0) == (iota((128, SLOTS), 1) & 31))
    mine = iota((N_SEQ, SLOTS), 0) == (iota((N_SEQ, SLOTS), 1) >> 5)
    row_hi = nn((got >> 4).astype(F32).astype(BF16), spread)
    row_lo = nn((got & 15).astype(F32).astype(BF16), spread)
    row = jnp.sum(jnp.where(mine, row_hi * 16.0 + row_lo, 0.0), axis=0, keepdims=True).astype(jnp.int32)
    for j in range(ROWS // 128):
        onehot_u[j * 128 : (j + 1) * 128, :] = hot(iota((128, SLOTS), 0) + j * 128 == row)
    row_b = jnp.broadcast_to(row.astype(F32), (128, SLOTS))
    for j in range(SLOTS // 128):
        col = jnp.transpose(row_b[:, j * 128 : (j + 1) * 128]).astype(jnp.int32)
        for k in range(ROWS // 128):
            onehot_ut[j * 128 : (j + 1) * 128, k * 128 : (k + 1) * 128] = hot(iota((128, 128), 1) + k * 128 == col)

    wait_recv(recv_a.at[others], 0)
    serial = nn(onehot_u[...], recv_a[...])
    center = serial - jnp.mean(serial, axis=1, keepdims=True)
    inv = lax.rsqrt(jnp.mean(center * center, axis=1, keepdims=True) + 1e-05)
    standard = center * inv
    xhat[...] = standard
    invs[...] = jnp.broadcast_to(inv, (ROWS, 128))
    normed_f = (standard * gain_ref[...]).astype(BF16)
    normed_t[...] = jnp.transpose(normed_f)
    loads[2].wait()
    qkv[...] = nn(normed_f, wqkv_ref[...]).astype(BF16)

    low = iota((ROWS, 128), 1) < HD

    def cols(base, p):
        return pl.ds(pl.multiple_of(base + p * 128, 128), 128)

    def half(x, h):
        return jnp.where(low if h == 0 else ~low, x.astype(F32), 0.0)

    def forward(p, _):
        q, k, v = qkv[:, cols(0, p)], qkv[:, cols(C, p)], qkv[:, cols(2 * C, p)]
        v_t = jnp.transpose(v)
        for h in range(2):
            scores = nt((half(k, h) * SCALE).astype(BF16), q)
            expo = jnp.exp(scores - jnp.max(scores, axis=0, keepdims=True))
            prob = expo * (1.0 / jnp.sum(expo, axis=0, keepdims=True))
            probs[2 * p + h] = prob
            rows = pl.ds(pl.multiple_of(p * 128 + h * HD, HD), HD)
            attn_t[rows, :] = nn(v_t[h * HD : (h + 1) * HD], prob.astype(BF16)).astype(BF16)
        return 0

    lax.fori_loop(0, PAIRS, forward, 0)

    wait_recv(recv_b.at[others], 1)
    sgrad[...] = nn(onehot_u[...], recv_b[...]).astype(BF16)
    loads[3].wait()
    dattn[...] = nt(sgrad[...], wproj_ref[...]).astype(BF16)

    def values_part(c, hook):
        for k in range(2):
            p = 2 * c + k
            at = slice(p * 128, (p + 1) * 128)
            dv = [nn(probs[2 * p + h].astype(BF16), dattn[:, at]) for h in range(2)]
            dv = jnp.where(low, dv[0], dv[1]).astype(BF16)
            dqkv[:, 2 * C + p * 128 : 2 * C + (p + 1) * 128] = dv
            grads[c, k * C : (k + 1) * C, :] = nn(normed_t[...], dv)
            if k == 0:
                hook()
            proj = nn(attn_t[at, :], sgrad[...])
            for j in range(4):
                grads[c, (2 + k) * C + j * 128 : (2 + k) * C + (j + 1) * 128, :] = proj[:, j * 128 : (j + 1) * 128]

    def keys_part(c, hook):
        for k in range(2):
            p = 2 * c + k
            at = slice(p * 128, (p + 1) * 128)
            q, keys, v = qkv[:, at], qkv[:, C + p * 128 : C + (p + 1) * 128], qkv[:, 2 * C + p * 128 : 2 * C + (p + 1) * 128]
            k_t = jnp.transpose(keys)
            dq_t, dk = [], []
            for h in range(2):
                prob = probs[2 * p + h]
                d_prob = nt(half(v, h).astype(BF16), dattn[:, at])
                delta = jnp.sum(d_prob * prob, axis=0, keepdims=True)
                d_score = (prob * (d_prob - delta) * SCALE).astype(BF16)
                dq_t.append(nn(k_t[h * HD : (h + 1) * HD], d_score))
                dk.append(nn(d_score, q))
            dq = jnp.transpose(jnp.concatenate(dq_t, axis=0)).astype(BF16)
            dk = jnp.where(low, dk[0], dk[1]).astype(BF16)
            for n, part in enumerate((dq, dk)):
                dqkv[:, n * C + p * 128 : n * C + (p + 1) * 128] = part
                grads[2 + c, (2 * k + n) * C : (2 * k + n + 1) * C, :] = nn(normed_t[...], part)
            if k == 0:
                hook()

    def span(start, n):
        return pl.ds(pl.multiple_of(start, 8), n)

    core = me["seq_2"]
    half_rows = CHUNK // 2
    COLORS = (("seq_0", "seq_1"), ("seq_1", "seq_0"))

    def place(color, level):
        first, second = COLORS[color]
        at = core * half_rows + color * 512
        if level > 0:
            at = at + me[first] * 128
        if level > 1:
            at = at + me[second] * 32
        return at

    def r_wait_recv(ref, stage, p):
        remote(ref, ref, r_send.at[stage, p], r_recv.at[stage, p], here).wait_recv()

    def r_wait_send(ref, stage, p):
        remote(ref, ref, r_send.at[stage, p], r_recv.at[stage, p], here).wait_send()

    def r_start(src, dst, stage, p, axis, t):
        remote(src, dst, r_send.at[stage, p], r_recv.at[stage, p], {axis: t}).start()

    def s_core(p):
        r_start(grads.at[p, span((1 - core) * half_rows, half_rows)], core_buf.at[p], 0, p, "seq_2", 1 - core)

    def s_first(p):
        r_wait_recv(core_buf.at[p], 0, p)
        acc[p] = grads[p, span(core * half_rows, half_rows), :] + core_buf[p]
        for d in range(3):
            for color, (first, _) in enumerate(COLORS):
                t = peers(first)[d]
                r_start(acc.at[p, span(color * 512 + t * 128, 128)], first_buf.at[p, color, d], 1, p, first, t)

    def s_second(p):
        r_wait_recv(first_buf.at[p], 1, p)
        for color, (first, _) in enumerate(COLORS):
            got = first_buf[p, color, 0] + first_buf[p, color, 1] + first_buf[p, color, 2]
            acc2[p, color * 128 : (color + 1) * 128, :] = acc[p, span(color * 512 + me[first] * 128, 128), :] + got
        for d in range(3):
            for color, (_, second) in enumerate(COLORS):
                t = peers(second)[d]
                r_start(acc2.at[p, span(color * 128 + t * 32, 32)], second_buf.at[p, color, d], 2, p, second, t)

    def s_z(p):
        r_wait_recv(second_buf.at[p], 2, p)
        for color, (_, second) in enumerate(COLORS):
            got = second_buf[p, color, 0] + second_buf[p, color, 1] + second_buf[p, color, 2]
            acc3[p, color * 32 : (color + 1) * 32, :] = acc2[p, span(color * 128 + me[second] * 32, 32), :] + got
        for d, t in enumerate(peers("dp")):
            r_start(acc3.at[p, span(t * 8, 8)], z_buf.at[p, d], 3, p, "dp", t)

    z = me["dp"]
    z_color, z_block = z // 4, lax.rem(z, 4)
    z_place = (1 - z_color) * place(0, 2) + z_color * place(1, 2) + z_block * 8

    def s_gather_z(p):
        r_wait_recv(z_buf.at[p], 3, p)
        total = acc3[p, span(z * 8, 8), :]
        for d in range(7):
            total = total + z_buf[p, d]
        own = span(z_place, 8)
        res[p, own, :] = total.astype(BF16)
        for t in peers("dp"):
            r_start(res.at[p, own], res.at[p, own], 4, p, "dp", t)

    def s_gather_second(p):
        r_wait_recv(res.at[p, pl.ds(0, 56)], 4, p)
        for d in range(3):
            for color, (_, second) in enumerate(COLORS):
                own = span(place(color, 2), 32)
                r_start(res.at[p, own], res.at[p, own], 5, p, second, peers(second)[d])

    def s_gather_first(p):
        r_wait_recv(res.at[p, pl.ds(0, 192)], 5, p)
        for d in range(3):
            for color, (first, _) in enumerate(COLORS):
                own = span(place(color, 1), 128)
                r_start(res.at[p, own], res.at[p, own], 6, p, first, peers(first)[d])

    def s_gather_core(p):
        r_wait_recv(res.at[p, pl.ds(0, 768)], 6, p)
        own = span(core * half_rows, half_rows)
        r_start(res.at[p, own], res.at[p, own], 7, p, "seq_2", 1 - core)

    def finish(p):
        r_wait_recv(res.at[p, pl.ds(0, half_rows)], 7, p)

    def gain_stage(k, axis, buf, value):
        m = me[axis]
        buf[m] = value
        for t in peers(axis):
            remote(buf.at[m], buf.at[m], g_send.at[k], g_recv.at[k], {axis: t}).start()

    def gain_sum(k, axis, buf):
        n = AXES[axis]
        ref = buf.at[pl.ds(0, n - 1)]
        copy = remote(ref, ref, g_send.at[k], g_recv.at[k], here)
        copy.wait_recv()
        copy.wait_send()
        total = buf[0]
        for j in range(1, n):
            total = total + buf[j]
        return total

    values_part(0, lambda: None)
    s_core(0)
    values_part(1, lambda: s_first(0))
    s_core(1)
    keys_part(0, lambda: s_first(1))
    s_core(2)
    keys_part(1, lambda: s_first(2))
    s_core(3)

    d_normed = nt(dqkv[...], wqkv_ref[...])
    s_first(3)
    standard = xhat[...]
    gg = jnp.sum(d_normed * standard, axis=0, keepdims=True)
    for j in range(8):
        gg_ref[j : j + 1, :] = gg[:, j * 128 : (j + 1) * 128] if j < 4 else jnp.zeros((1, 128), F32)
    gain_stage(0, "seq_2", g_core, gg_ref[...])
    scaled = d_normed * gain_ref[...]
    first = jnp.mean(scaled, axis=1, keepdims=True)
    second = jnp.mean(scaled * standard, axis=1, keepdims=True)
    dx = (sgrad[...].astype(F32) + invs[:, 0:1] * (scaled - first - standard * second)).astype(BF16)
    wait_send(send_a.at[others], 0)
    send_a[...] = nn(onehot_ut[...], dx).astype(BF16)
    back[0:CAP, :] = send_a[0:CAP, :]
    gain_stage(1, "seq_0", g_x, gain_sum(0, "seq_2", g_core))
    for p in range(PAIRS):
        s_second(p)
    send_all(send_a, back, 3, -1, FAR_FIRST[:8])
    for p in range(PAIRS):
        s_z(p)
    send_all(send_a, back, 3, -1, FAR_FIRST[8:18])
    gain_stage(2, "seq_1", g_y, gain_sum(1, "seq_0", g_x))
    for p in range(PAIRS):
        s_gather_z(p)
    send_all(send_a, back, 3, -1, FAR_FIRST[18:28])
    for p in range(PAIRS):
        s_gather_second(p)
    send_all(send_a, back, 3, -1, FAR_FIRST[28:])
    gain_stage(3, "dp", g_z, gain_sum(2, "seq_1", g_y))
    for p in range(PAIRS):
        s_gather_first(p)
    for p in range(PAIRS):
        s_gather_core(p)
    wait_recv(back.at[others], 3)
    out_ref[...] = nn(onehot_pt[...], back[...]).astype(BF16)
    gg_ref[...] = gain_sum(3, "dp", g_z)
    for p in range(PAIRS):
        finish(p)
    wait_send(pos_recv.at[pl.ds(1, N_SEQ - 1)], 2)
    wait_send(send_b.at[others], 1)
    wait_send(send_a.at[others], 3)
    sent = (half_rows, 768, 192, 56, 56, 192, 768, half_rows)
    for p in range(PAIRS):
        for stage in range(8):
            r_wait_send((grads if stage < 4 else res).at[p, pl.ds(0, sent[stage])], stage, p)


def vmem(shape, dtype=F32):
    return pltpu.VMEM(shape, dtype)


DMA = pltpu.SemaphoreType.DMA
VSPEC = pl.BlockSpec(memory_space=pltpu.VMEM)
HBM = pl.BlockSpec(memory_space=pltpu.HBM)


def widen_kernel(res_ref, rows_ref, gg_ref, pts_out, qkv_out, proj_out, gain_out, wide, wide_p, sem):
    copies = [pltpu.make_async_copy(rows_ref, pts_out.at[0], sem.at[0])]
    copies[0].start()
    for r in range(4):
        at = slice(r * 128, (r + 1) * 128)
        for p in range(PAIRS):
            lanes = slice(p * 128, (p + 1) * 128)
            c, k = p // 2, p % 2
            for n, (chunk, row) in enumerate(((2 + c, 2 * k), (2 + c, 2 * k + 1), (c, k))):
                start = row * C + r * 128
                wide[at, n * C + p * 128 : n * C + (p + 1) * 128] = res_ref[chunk, start : start + 128, :].astype(F32)
            start = (2 + r % 2) * C + p * 128
            wide_p[at, lanes] = res_ref[r // 2, start : start + 128, :].astype(F32)
        rows = pl.ds(r * 128, 128)
        copies.append(pltpu.make_async_copy(wide.at[rows], qkv_out.at[rows], sem.at[1 + r]))
        copies.append(pltpu.make_async_copy(wide_p.at[rows], proj_out.at[rows], sem.at[5 + r]))
        copies[-2].start()
        copies[-1].start()
    for j in range(4):
        gain_out[:, j * 128 : (j + 1) * 128] = gg_ref[j : j + 1, :]
    for copy in copies:
        copy.wait()


def per_device(points, cotangent, dest, w_qkv, w_proj, gain):
    big = lambda: vmem((SLOTS, C), BF16)
    grad_local, res, gg = pl.pallas_call(
        block_kernel,
        name="block",
        out_shape=(
            vmem((ROWS, C), BF16),
            vmem((PAIRS, CHUNK, 128), BF16),
            vmem((8, 128)),
        ),
        in_specs=[VSPEC, HBM, HBM, HBM, HBM, VSPEC],
        out_specs=(VSPEC,) * 3,
        scratch_shapes=[
            big(), big(), big(), big(), big(),
            vmem((N_SEQ, 1, 128)), vmem((N_SEQ, 1, 128)), vmem((N_SEQ, 128)),
            vmem((ROWS, 3 * C), BF16), vmem((ROWS, C), BF16), vmem((ROWS, C), BF16),
            vmem((ROWS, C)), vmem((ROWS, 128)), vmem((C, ROWS), BF16), vmem((ROWS, 3 * C), BF16),
            vmem((C, ROWS), BF16), vmem((HEADS, ROWS, ROWS)),
            vmem((ROWS, SLOTS), BF16), vmem((SLOTS, ROWS), BF16), vmem((ROWS, SLOTS), BF16),
            vmem((PAIRS, CHUNK, 128)), vmem((PAIRS, CHUNK // 2, 128)),
            vmem((PAIRS, 256, 128)), vmem((PAIRS, 64, 128)), vmem((PAIRS, CHUNK // 2, 128)),
            vmem((PAIRS, 2, 3, 128, 128)), vmem((PAIRS, 2, 3, 32, 128)), vmem((PAIRS, 7, 8, 128)),
            vmem((2, 8, 128)), vmem((4, 8, 128)), vmem((4, 8, 128)), vmem((8, 8, 128)),
            vmem((ROWS, C), BF16), vmem((ROWS, C), BF16), vmem((C, 3 * C), BF16), vmem((C, C), BF16),
            DMA((4,)), DMA((4,)), DMA((8, PAIRS)), DMA((8, PAIRS)), DMA((4,)), DMA((4,)), DMA((4,)),
        ],
        compiler_params=pltpu.CompilerParams(
            collective_id=0, has_side_effects=True, vmem_limit_bytes=56 * 2**20
        ),
    )(dest, points[0], cotangent[0], w_qkv, w_proj, gain[None, :])
    grad_points, grad_qkv, grad_proj, gain_gradient = pl.pallas_call(
        widen_kernel,
        name="widen",
        out_shape=(
            jax.ShapeDtypeStruct((1, ROWS, C), BF16),
            jax.ShapeDtypeStruct((C, 3 * C), F32),
            jax.ShapeDtypeStruct((C, C), F32),
            jax.ShapeDtypeStruct((1, C), F32),
        ),
        in_specs=[VSPEC] * 3,
        out_specs=(HBM, HBM, HBM, VSPEC),
        scratch_shapes=[vmem((C, 3 * C)), vmem((C, C)), DMA((9,))],
        compiler_params=pltpu.CompilerParams(vmem_limit_bytes=16 * 2**20),
    )(res, grad_local, gg)
    return (grad_points, grad_qkv, grad_proj, gain_gradient.reshape(C))


def solution(mesh):
    finer = Mesh(mesh.devices.reshape(4, 4, 2, mesh.shape["dp"]), ("seq_0", "seq_1", "seq_2", "dp"))
    placed = (P("dp", SEQ, None), P("dp", SEQ, None), P("dp", SEQ), P(), P(), P())
    return jax.shard_map(
        per_device,
        mesh=finer,
        in_specs=placed,
        out_specs=(P("dp", SEQ, None), P(), P(), P()),
        check_vma=False,
    )
```

profile of v0, /device:TPU:1, one launch (start us, length us, event | category | flops | bytes accessed | tf_op | source)
XLA Modules:
  0.0 95.6 jit_solution(11776439151210328890)
XLA Ops:
  0.6 92.0 %block.1 = (bf16[512,512]{1,0:T(8,128)(2,1)S(1)}, bf16[4,2048,128]{2,1,0:T(8,128)(2,1)S(1)}, f32[8,128]{1,0:T(8,128)S(1)}) custom-call(s32[1,512]{1,0:T(1,128)} %dest_ref.1, bf16[512,512]{1,0:T(8,128)(2,1)} %bitcast.4, bf16[512,512]{1,0:T(8,128)(2,1)} %bitcast.5, bf16[512,1536]{1,0:T(8,128)(2,1)} %wqkv_hbm.1, bf16[512,512]{1,0:T(8,128)(2,1)} %wproj_hbm.1, ...), custom_call_target="tpu_custom_call" | custom-call | tf_op jit(solution)/shard_map/block/pallas_call | solution.py:434
  92.6 2.8 %widen.1 = (bf16[1,512,512]{2,1,0:T(8,128)(2,1)}, f32[512,1536]{1,0:T(8,128)}, f32[512,512]{1,0:T(8,128)}, f32[1,512]{1,0:T(1,128)}) custom-call(bf16[4,2048,128]{2,1,0:T(8,128)(2,1)S(1)} %get-tuple-element.11.res_ref, bf16[512,512]{1,0:T(8,128)(2,1)S(1)} %get-tuple-element.12.rows_ref, f32[8,128]{1,0:T(8,128)S(1)} %get-tuple-element.13.gg_ref), custom_call_target="tpu_custom_call" | custom-call | tf_op jit(solution)/shard_map/widen/pallas_call | solution.py:462
where the time goes:
time: 95.7 us; the launch traced here: 95.6 us
  Pallas kernels  94.8 us (99%)
    pallas_call x1, Pallas kernels, per_device(): pl.pallas_call(block_kernel, name='block', out_shape=(vmem((ROWS, C), BF1...  92 us
    pallas_call x1, Pallas kernels, per_device(): pl.pallas_call(widen_kernel, name='widen', out_shape=(jax.ShapeDtypeStruc...  2.83 us

commit v1 on v0

--- a/solution.py
+++ b/solution.py
@@ -366,20 +366,19 @@
     gain_stage(1, "seq_0", g_x, gain_sum(0, "seq_2", g_core))
     for p in range(PAIRS):
         s_second(p)
-    send_all(send_a, back, 3, -1, FAR_FIRST[:8])
     for p in range(PAIRS):
         s_z(p)
-    send_all(send_a, back, 3, -1, FAR_FIRST[8:18])
+    send_all(send_a, back, 3, -1, FAR_FIRST[0:12])
     gain_stage(2, "seq_1", g_y, gain_sum(1, "seq_0", g_x))
     for p in range(PAIRS):
         s_gather_z(p)
-    send_all(send_a, back, 3, -1, FAR_FIRST[18:28])
+    send_all(send_a, back, 3, -1, FAR_FIRST[12:23])
     for p in range(PAIRS):
         s_gather_second(p)
-    send_all(send_a, back, 3, -1, FAR_FIRST[28:])
     gain_stage(3, "dp", g_z, gain_sum(2, "seq_1", g_y))
     for p in range(PAIRS):
         s_gather_first(p)
+    send_all(send_a, back, 3, -1, FAR_FIRST[23:31])
     for p in range(PAIRS):
         s_gather_core(p)
     wait_recv(back.at[others], 3)

time: 95.7 us -> 93.1 us (0.973)
  Pallas kernels: 94.8 us -> 92.2 us
    pallas_call x1, Pallas kernels: 92 us -> 89.3 us  [per_device(): pl.pallas_call(block_kernel, name='block', out_shape=(vmem((ROWS, C), BF1...]
where the time goes in v1:
time: 93.1 us; the launch traced here: 93 us
  Pallas kernels  92.2 us (99%)
    pallas_call x1, Pallas kernels, per_device(): pl.pallas_call(block_kernel, name='block', out_shape=(vmem((ROWS, C), BF1...  89.3 us
    pallas_call x1, Pallas kernels, per_device(): pl.pallas_call(widen_kernel, name='widen', out_shape=(jax.ShapeDtypeStruc...  2.83 us

profile of v1, /device:TPU:1, one launch (start us, length us, event | category | flops | bytes accessed | tf_op | source)
XLA Modules:
  0.0 93.0 jit_solution(11643720270511237886)
XLA Ops:
  0.6 89.3 %block.1 = (bf16[512,512]{1,0:T(8,128)(2,1)S(1)}, bf16[4,2048,128]{2,1,0:T(8,128)(2,1)S(1)}, f32[8,128]{1,0:T(8,128)S(1)}) custom-call(s32[1,512]{1,0:T(1,128)} %dest_ref.1, bf16[512,512]{1,0:T(8,128)(2,1)} %bitcast.4, bf16[512,512]{1,0:T(8,128)(2,1)} %bitcast.5, bf16[512,1536]{1,0:T(8,128)(2,1)} %wqkv_hbm.1, bf16[512,512]{1,0:T(8,128)(2,1)} %wproj_hbm.1, ...), custom_call_target="tpu_custom_call" | custom-call | tf_op jit(solution)/shard_map/block/pallas_call | solution.py:433
  90.0 2.8 %widen.1 = (bf16[1,512,512]{2,1,0:T(8,128)(2,1)}, f32[512,1536]{1,0:T(8,128)}, f32[512,512]{1,0:T(8,128)}, f32[1,512]{1,0:T(1,128)}) custom-call(bf16[4,2048,128]{2,1,0:T(8,128)(2,1)S(1)} %get-tuple-element.11.res_ref, bf16[512,512]{1,0:T(8,128)(2,1)S(1)} %get-tuple-element.12.rows_ref, f32[8,128]{1,0:T(8,128)S(1)} %get-tuple-element.13.gg_ref), custom_call_target="tpu_custom_call" | custom-call | tf_op jit(solution)/shard_map/widen/pallas_call | solution.py:461
